TPU v7x, 32 devices: a whole 2x2x4 slice. The times are simulated.
32 devices in a mesh: row: 8 (over y, x, core), col: 4 (over z).
Axes of the slice: x: 2, y: 2, z: 4, core: 2. Of those that a mesh axis runs over, the one named last changes fastest.
Arguments:
- descriptors: bfloat16 [32, 6144], P(None, ('row', 'col')), may hold values from -6 to 6
- densities: float32 [6144], P(('row', 'col')), may hold values from 0.25 to 4
- vectors: float32 [32, 6144], P(None, ('row', 'col')), may hold values from -6 to 6
Outputs:
- next_block: float32 [32, 6144], P(None, ('row', 'col'))
All inputs are finite; a program needn't handle non-finite values.
Results may differ from a plain program's by a relative error of at most 0.0036.
Values may be sent and summed in bfloat16 or wider, within the bound.
No kernel may reach another device: no remote copies, remote signals or barrier semaphores. Data moves between devices by JAX's collectives and lax.ppermute only.
A program may use at most 64 MiB of HBM per device.

v0:
```python
import math
import jax
import jax.numpy as jnp
from jax import lax
from jax.sharding import PartitionSpec as P

kernel_width = 8.0


def tile_terms(targets, target_norm, piece):
    piece_feat, piece_vals, piece_inv = piece
    piece_norm = jnp.sum(jnp.square(piece_feat.astype(jnp.float32)), axis=0)
    feature_dim, target_count = targets.shape
    span_rows = math.gcd(target_count, 512)
    block_count = target_count // span_rows
    blocks = targets.reshape(feature_dim, block_count, span_rows).transpose(1, 0, 2)
    norm_blocks = target_norm.reshape(block_count, span_rows)

    def tile_block(block_item):
        block_feat, block_norm = block_item
        inner_prod = lax.dot_general(
            block_feat, piece_feat, (((0,), (0,)), ((), ())), preferred_element_type=jnp.float32
        )
        kernel = jnp.exp(
            -(block_norm[:, None] + piece_norm[None, :] - 2.0 * inner_prod) / kernel_width
        ).astype(jnp.bfloat16)
        numerator = lax.dot_general(
            piece_vals, kernel, (((1,), (1,)), ((), ())), preferred_element_type=jnp.float32
        )
        degree = lax.dot_general(
            piece_inv, kernel, (((1,), (1,)), ((), ())), preferred_element_type=jnp.float32
        )
        return (numerator, degree)

    numerator, degree = lax.map(tile_block, (blocks, norm_blocks))
    numerator = numerator.transpose(1, 0, 2).reshape(piece_vals.shape[0], target_count)
    degree = degree.transpose(1, 0, 2).reshape(1, target_count)
    return (numerator, degree)


def accumulate(targets, vec_count):
    target_norm = jnp.sum(jnp.square(targets.astype(jnp.float32)), axis=0)

    def fold_piece(running, piece, start):
        numerator, degree = tile_terms(targets, target_norm, piece)
        return (numerator, degree)

    initial = (
        jnp.zeros((vec_count, targets.shape[1]), jnp.float32),
        jnp.zeros((1, targets.shape[1]), jnp.float32),
    )
    return (fold_piece, initial)


def per_device(descriptors, densities, vectors):
    highest = lax.Precision.HIGHEST
    vec_count = vectors.shape[0]
    weighted = (vectors / densities[None, :]).astype(jnp.bfloat16)
    inverse = (1.0 / densities).astype(jnp.bfloat16)[None, :]
    targets = lax.all_gather(descriptors, "col", axis=1, tiled=True)
    fold_piece, initial = accumulate(targets, vec_count)
    partial_value = fold_piece(
        initial,
        (
            lax.all_gather(descriptors, "row", axis=1, tiled=True),
            lax.all_gather(weighted, "row", axis=1, tiled=True),
            lax.all_gather(inverse, "row", axis=1, tiled=True),
        ),
        jnp.int32(0),
    )
    numerator, degree = (
        lax.psum_scatter(partial_value[0], "col", scatter_dimension=1, tiled=True),
        lax.psum_scatter(partial_value[1], "col", scatter_dimension=1, tiled=True),
    )
    diffused = numerator / degree
    samples_float = float(descriptors.shape[1] * lax.axis_size("row") * lax.axis_size("col"))
    coupling, diffused_gram, basis_gram = lax.psum(
        (
            jnp.dot(vectors, diffused.T, precision=highest),
            jnp.dot(diffused, diffused.T, precision=highest),
            jnp.dot(vectors, vectors.T, precision=highest),
        ),
        ("row", "col"),
    )
    remainder = diffused - jnp.dot(coupling.T, vectors, precision=highest) / samples_float
    cross_term = jnp.dot(coupling.T, coupling, precision=highest)
    basis_term = jnp.dot(
        coupling.T, jnp.dot(basis_gram, coupling, precision=highest), precision=highest
    )
    spread = (
        diffused_gram
        - 2.0 * cross_term / samples_float
        + basis_term / (samples_float * samples_float)
    )
    factor = jnp.linalg.cholesky(spread)
    solved = jax.scipy.linalg.solve_triangular(factor, remainder, lower=True)
    return math.sqrt(samples_float) * solved


def solution(mesh):
    return jax.shard_map(
        per_device,
        mesh=mesh,
        in_specs=(P(None, ("row", "col")), P(("row", "col")), P(None, ("row", "col"))),
        out_specs=P(None, ("row", "col")),
        check_vma=False,
    )
```

profile of v0, /device:TPU:0, one launch (start us, length us, event | category | flops | bytes accessed | tf_op | source)
XLA Modules:
  0.0 157.3 jit_solution(3891402411580507994)
XLA Ops:
  6.5 0.0 reduce-scatter.9.cloned.1.call-start
  6.5 11.0 %all-gather.2 = bf16[8,192,32]{1,2,0:T(8,128)(2,1)S(1)} all-gather(bf16[1,192,32]{1,2,0:T(8,128)(2,1)} %bitcast.102), channel_id=1, replica_groups=mesh['row'=8,'col'=4] {'row'}, dimensions={0}, use_global_device_ids=true | all-gather | bytes 110592 | tf_op jit(solution)/shard_map/all_gather | solution.py:65
  17.5 13.6 %all-gather.1 = bf16[4,192,32]{1,2,0:T(8,128)(2,1)S(1)} all-gather(bf16[1,192,32]{1,2,0:T(8,128)(2,1)} %bitcast.103), channel_id=1, replica_groups=mesh['row'=8,'col'=4] {'col'}, dimensions={0}, use_global_device_ids=true | all-gather | bytes 61440 | tf_op jit(solution)/shard_map/all_gather | solution.py:60
  31.1 0.1 copy.27
  31.2 0.0 copy-start.2
  31.2 0.1 reshape.38
  31.4 0.1 copy.26
  31.4 0.1 reshape.36
  31.6 0.0 copy-done.1
  31.7 9.0 %all-gather.3 = bf16[8,192,32]{1,2,0:T(8,128)(2,1)S(1)} all-gather(bf16[1,192,32]{1,2,0:T(8,128)(2,1)S(1)} %fusion.17), channel_id=1, replica_groups=mesh['row'=8,'col'=4] {'row'}, dimensions={0}, use_global_device_ids=true | all-gather | bytes 110592 | tf_op jit(solution)/shard_map/all_gather | solution.py:66
  40.7 0.1 copy.28
  40.8 0.1 reshape.40
  40.9 0.6 dynamic-slice
  42.2 0.2 dynamic-update-slice.3
  42.4 13.2 %all-reduce = bf16[1536]{0:T(1024)(128)(2,1)S(1)} all-reduce(bf16[1536]{0:T(1024)(128)(2,1)S(1)} %dynamic-update-slice.3), channel_id=2, replica_groups=mesh['row'=8,'col'=4] {'row'}, use_global_device_ids=true, to_apply=%add | all-reduce | flops 1536 | bytes 6144
  55.6 3.6 %while.12 = (s32[]{:T(128)}, f32[3,32,256]{2,1,0:T(8,128)S(1)}, f32[3,1,256]{2,1,0:T(1,128)S(1)}, f32[3,256]{1,0:T(4,128)S(1)}, f32[1536]{0:T(1024)S(1)}, /*inde...) while((s32[]{:T(128)}, f32[3,32,256]{2,1,0:T(8,128)S(1)}, ...), condition=%wide.region_3.4_spmd, body=%wide.region_2.3_spmd.sunk | while | flops 53477376 | bytes 2623605 | solution.py:35
  55.7 0.5 fusion.52
  56.2 0.3 fusion.53
  56.5 0.3 fusion.54
  56.8 0.6 fusion.52
  57.4 0.3 fusion.53
  57.7 0.3 fusion.54
  58.0 0.6 fusion.52
  58.6 0.3 fusion.53
  58.9 0.3 fusion.54
  59.2 1.0 copy.40
  60.2 0.0 reduce-scatter.9.cloned.1.call-update
  60.2 0.0 reduce-scatter.7.cloned.1.call-start
  60.3 0.9 copy.42
  61.2 0.0 reduce-scatter.7.cloned.1.call-update
  61.2 0.2 fusion.19
  61.4 19.1 %reduce-scatter.9.cloned.1.call-done = f32[192,1]{1,0:T(8,128)} async-done(((f32[768,1]{1,0:T(8,128)}), f32[192,1]{1,0:T(8,128)}) %reduce-scatter.9.cloned.1.call-update) | async-done | bytes 784
  80.4 1.0 copy.41
  81.4 20.4 %reduce-scatter.7.cloned.1.call-done = f32[192,32]{1,0:T(8,128)} async-done(((f32[768,32]{1,0:T(8,128)}), f32[192,32]{1,0:T(8,128)}) %reduce-scatter.7.cloned.1.call-update) | async-done | bytes 24592
  101.8 1.0 copy.39
  102.8 0.2 fusion.18
  103.0 0.2 convolution_bitcast_fusion.2
  103.1 39.0 %all-reduce.1 = (f32[32,32]{0,1:T(8,128)S(1)}, f32[32,32]{0,1:T(8,128)S(1)}, f32[32,32]{1,0:T(8,128)S(1)}) all-reduce(f32[32,32]{0,1:T(8,128)S(1)} %convolution_bitcast_fusion.2, f32[32,32]{0,1:T(8,128)S(1)} %fusion.18, f32[32,32]{1,0:T(8,128)S(1)} %fusion.19), channel_id=1, replica_groups=mesh['row'=8,'col'=4] {'row','col'}, use_global_device_ids=true, to_apply=%region_7.8 | all-reduce | flops 3072 | bytes 24576 | tf_op jit(solution)/shard_map/psum | solution.py:77
  142.1 0.2 fusion.11
  142.3 0.1 fusion.20
  142.4 0.2 fusion.13
  142.6 0.2 fusion.12
  142.8 0.1 copy.34
  142.9 2.9 %cholesky.16 = f32[32,32]{1,0:T(8,128)S(1)} custom-call(f32[32,32]{1,0:T(8,128)S(1)} %fusion.16), custom_call_target="Cholesky" | custom-call | tf_op jit(solution)/shard_map/jit(cholesky)/cholesky | solution.py:95
  145.8 0.6 compare_reduce_fusion
  146.5 0.7 fusion.14
  147.1 2.4 %custom-call.7 = f32[1,32,32]{1,2,0:T(8,128)S(1)} custom-call(f32[1,32,32]{2,1,0:T(8,128)S(1)} %fusion.14), custom_call_target="InvertDiagBlocksLowerTriangular" | custom-call | tf_op jit(solution)/shard_map/jit(_solve_triangular)/triangular_solve | solution.py:96
  149.6 0.9 convolution_multiply_fusion.1
  (20 shorter events, 0.2 us)
Async XLA Ops:
  6.5 25.1 %copy-start.1 = (f32[192]{0:T(256)S(1)}, f32[192]{0:T(256)}, u32[]{:S(2)}) copy-start(f32[192]{0:T(256)} %param.6) | copy-start | bytes 2308
  6.5 25.1 %copy-start = (f32[32,192]{1,0:T(8,128)S(1)}, f32[32,192]{1,0:T(8,128)}, u32[]{:S(2)}) copy-start(f32[32,192]{1,0:T(8,128)} %param.7) | copy-start | bytes 73732
  6.5 73.9 %reduce-scatter.9.cloned.1.call-start = ((), (), s32[]{:S(2)}) async-start(), calls=%async_computation.3 | async-start | bytes 491520
  31.2 9.8 %copy-start.2 = (u32[32]{0:T(128)S(1)}, u32[32]{0:T(128)}, u32[]{:S(2)}) copy-start(u32[32]{0:T(128)} %constant.83) | copy-start | bytes 388
  60.2 41.6 %reduce-scatter.7.cloned.1.call-start = ((), (), s32[]{:S(2)}) async-start(), calls=%async_computation.2 | async-start | bytes 491520
Sparse Core Ops, SparseCore 0:
  60.3 20.0 reduce-scatter.8
  82.7 19.0 reduce-scatter.6
where the time goes:
time: 158 us; the launch traced here: 157 us
  blocking collectives  85.7 us (54%)
  waiting for transfers between devices  39.5 us (25%)
  between operations  14.2 us (9%)
  other arithmetic  6.76 us (4%)
  matrix products  5.55 us (4%)
  local copies, waits for them, and re-layouts  5.41 us (3%)
    unnamed x4, waiting for transfers between devices  39.5 us
    psum x1, blocking collectives, per_device(): lax.psum((jnp.dot(vectors, diffused.T, precision=highest), jnp.dot(diffus...  39 us
    all_gather x1, blocking collectives, per_device(): targets = lax.all_gather(descriptors, 'col', axis=1, tiled=True)  13.6 us
    unnamed x1, blocking collectives  13.2 us
    all_gather x1, blocking collectives, per_device(): lax.all_gather(descriptors, 'row', axis=1, tiled=True)  11 us
    all_gather x1, blocking collectives, per_device(): lax.all_gather(weighted, 'row', axis=1, tiled=True)  9.01 us
    unnamed x16, local copies, waits for them, and re-layouts  5.06 us
    another operation x3, other arithmetic, per_device(): factor = jnp.linalg.cholesky(spread)  3.6 us
  transfers between devices with their start and end apart: 2, of which 2 were waited for; matrix products, arithmetic and copies ran while one was open for 1% of the time, Pallas kernels for 0%

commit v1 on v0

--- a/solution.py
+++ b/solution.py
@@ -1,10 +1,20 @@
+import functools
 import math
 import jax
 import jax.numpy as jnp
 from jax import lax
 from jax.sharding import PartitionSpec as P
+from jax.lax import all_gather
 
 kernel_width = 8.0
+
+
+def order_row(field_in, link_axis, at_axis):
+    then = all_gather(field_in, link_axis)
+    return jnp.concatenate(then, axis=at_axis)
+
+
+report_rounds = functools.partial(order_row, link_axis="row", at_axis=1)
 
 
 def tile_terms(targets, target_norm, piece):
@@ -62,7 +72,7 @@
     partial_value = fold_piece(
         initial,
         (
-            lax.all_gather(descriptors, "row", axis=1, tiled=True),
+            report_rounds(descriptors),
             lax.all_gather(weighted, "row", axis=1, tiled=True),
             lax.all_gather(inverse, "row", axis=1, tiled=True),
         ),

time: 158 us -> 158 us (level)
    unnamed x16 -> x17, local copies, waits for them, and re-layouts: 5.06 us -> 4.92 us
where the time goes in v1:
time: 158 us; the launch traced here: 157 us
  blocking collectives  85.5 us (54%)
  waiting for transfers between devices  39.6 us (25%)
  between operations  14.3 us (9%)
  other arithmetic  6.81 us (4%)
  matrix products  5.55 us (4%)
  local copies, waits for them, and re-layouts  5.49 us (3%)
    unnamed x4, waiting for transfers between devices  39.6 us
    psum x1, blocking collectives, per_device(): lax.psum((jnp.dot(vectors, diffused.T, precision=highest), jnp.dot(diffus...  38.9 us
    all_gather x1, blocking collectives, per_device(): targets = lax.all_gather(descriptors, 'col', axis=1, tiled=True)  13.4 us
    unnamed x1, blocking collectives  13.2 us
    all_gather x1, blocking collectives, order_row(): then = all_gather(field_in, link_axis)  11 us
    all_gather x1, blocking collectives, per_device(): lax.all_gather(weighted, 'row', axis=1, tiled=True)  9.01 us
    unnamed x17, local copies, waits for them, and re-layouts  4.92 us
    another operation x3, other arithmetic, per_device(): factor = jnp.linalg.cholesky(spread)  3.6 us
  transfers between devices with their start and end apart: 2, of which 2 were waited for; matrix products, arithmetic and copies ran while one was open for 1% of the time, Pallas kernels for 0%

profile of v1, /device:TPU:0, one launch (start us, length us, event | category | flops | bytes accessed | tf_op | source)
XLA Modules:
  0.0 157.2 jit_solution(876172886935195600)
XLA Ops:
  6.5 11.0 %all-gather = bf16[256,192]{1,0:T(8,128)(2,1)S(1)} all-gather(bf16[32,192]{1,0:T(8,128)(2,1)} %param.5), channel_id=2, replica_groups=mesh['row'=8,'col'=4] {'row'}, dimensions={0}, use_global_device_ids=true | all-gather | bytes 110592 | tf_op jit(solution)/shard_map/all_gather | solution.py:13
  17.5 0.1 copy.48
  17.6 0.1 multiply_reduce_fusion
  17.7 0.0 copy-start.3
  17.8 0.1 reshape.38
  17.9 13.4 %all-gather.2 = bf16[4,192,32]{1,2,0:T(8,128)(2,1)S(1)} all-gather(bf16[1,192,32]{1,2,0:T(8,128)(2,1)S(1)} %bitcast.106), channel_id=1, replica_groups=mesh['row'=8,'col'=4] {'col'}, dimensions={0}, use_global_device_ids=true | all-gather | bytes 61440 | tf_op jit(solution)/shard_map/all_gather | solution.py:70
  31.3 0.1 copy.27
  31.3 0.1 reshape.46
  31.5 0.1 reduce_sum.22
  31.6 9.0 %all-gather.3 = bf16[8,192,32]{1,2,0:T(8,128)(2,1)S(1)} all-gather(bf16[1,192,32]{1,2,0:T(8,128)(2,1)S(1)} %fusion.17), channel_id=1, replica_groups=mesh['row'=8,'col'=4] {'row'}, dimensions={0}, use_global_device_ids=true | all-gather | bytes 110592 | tf_op jit(solution)/shard_map/all_gather | solution.py:76
  40.6 0.1 copy.29
  40.7 0.1 reshape.48
  40.9 0.6 dynamic-slice
  42.1 0.2 dynamic-update-slice.3
  42.4 13.2 %all-reduce = bf16[1536]{0:T(1024)(128)(2,1)S(1)} all-reduce(bf16[1536]{0:T(1024)(128)(2,1)S(1)} %dynamic-update-slice.3), channel_id=3, replica_groups=mesh['row'=8,'col'=4] {'row'}, use_global_device_ids=true, to_apply=%add | all-reduce | flops 1536 | bytes 6144
  55.6 3.6 %while.12 = (s32[]{:T(128)}, f32[3,32,256]{2,1,0:T(8,128)S(1)}, f32[3,1,256]{2,1,0:T(1,128)S(1)}, f32[3,256]{1,0:T(4,128)S(1)}, f32[1536]{0:T(1024)S(1)}, /*inde...) while((s32[]{:T(128)}, f32[3,32,256]{2,1,0:T(8,128)S(1)}, ...), condition=%wide.region_3.4_spmd, body=%wide.region_2.3_spmd.sunk | while | flops 53477376 | bytes 2623605 | solution.py:45
  55.6 0.5 fusion.52
  56.1 0.3 fusion.53
  56.4 0.3 fusion.54
  56.8 0.6 fusion.52
  57.3 0.3 fusion.53
  57.6 0.3 fusion.54
  58.0 0.6 fusion.52
  58.5 0.3 fusion.53
  58.8 0.3 fusion.54
  59.2 1.0 copy.41
  60.1 0.0 reduce-scatter.9.cloned.1.call-update
  60.2 0.0 reduce-scatter.7.cloned.1.call-start
  60.2 0.9 copy.43
  61.1 0.0 reduce-scatter.7.cloned.1.call-update
  61.2 0.2 fusion.19
  61.3 19.1 %reduce-scatter.9.cloned.1.call-done = f32[192,1]{1,0:T(8,128)} async-done(((f32[768,1]{1,0:T(8,128)}), f32[192,1]{1,0:T(8,128)}) %reduce-scatter.9.cloned.1.call-update) | async-done | bytes 784
  80.4 1.0 copy.42
  81.4 20.5 %reduce-scatter.7.cloned.1.call-done = f32[192,32]{1,0:T(8,128)} async-done(((f32[768,32]{1,0:T(8,128)}), f32[192,32]{1,0:T(8,128)}) %reduce-scatter.7.cloned.1.call-update) | async-done | bytes 24592
  101.8 1.0 copy.40
  102.8 0.2 fusion.18
  103.0 0.2 convolution_bitcast_fusion.2
  103.1 38.9 %all-reduce.1 = (f32[32,32]{0,1:T(8,128)S(1)}, f32[32,32]{0,1:T(8,128)S(1)}, f32[32,32]{1,0:T(8,128)S(1)}) all-reduce(f32[32,32]{0,1:T(8,128)S(1)} %convolution_bitcast_fusion.2, f32[32,32]{0,1:T(8,128)S(1)} %fusion.18, f32[32,32]{1,0:T(8,128)S(1)} %fusion.19), channel_id=1, replica_groups=mesh['row'=8,'col'=4] {'row','col'}, use_global_device_ids=true, to_apply=%region_7.8 | all-reduce | flops 3072 | bytes 24576 | tf_op jit(solution)/shard_map/psum | solution.py:87
  142.1 0.2 fusion.11
  142.2 0.1 fusion.20
  142.4 0.2 fusion.13
  142.6 0.2 fusion.12
  142.8 0.1 copy.35
  142.8 2.9 %cholesky.16 = f32[32,32]{1,0:T(8,128)S(1)} custom-call(f32[32,32]{1,0:T(8,128)S(1)} %fusion.16), custom_call_target="Cholesky" | custom-call | tf_op jit(solution)/shard_map/jit(cholesky)/cholesky | solution.py:105
  145.8 0.6 compare_reduce_fusion
  146.4 0.7 fusion.14
  147.1 2.4 %custom-call.7 = f32[1,32,32]{1,2,0:T(8,128)S(1)} custom-call(f32[1,32,32]{2,1,0:T(8,128)S(1)} %fusion.14), custom_call_target="InvertDiagBlocksLowerTriangular" | custom-call | tf_op jit(solution)/shard_map/jit(_solve_triangular)/triangular_solve | solution.py:106
  149.5 0.9 convolution_multiply_fusion.1
  (23 shorter events, 0.2 us)
Async XLA Ops:
  6.5 11.4 %copy-start.1 = (bf16[32,192]{1,0:T(8,128)(2,1)S(1)}, bf16[32,192]{1,0:T(8,128)(2,1)}, u32[]{:S(2)}) copy-start(bf16[32,192]{1,0:T(8,128)(2,1)} %param.5) | copy-start | bytes 36868
  6.5 25.1 %copy-start.2 = (f32[192]{0:T(256)S(1)}, f32[192]{0:T(256)}, u32[]{:S(2)}) copy-start(f32[192]{0:T(256)} %param.6) | copy-start | bytes 2308
  6.5 25.1 %copy-start = (f32[32,192]{1,0:T(8,128)S(1)}, f32[32,192]{1,0:T(8,128)}, u32[]{:S(2)}) copy-start(f32[32,192]{1,0:T(8,128)} %param.7) | copy-start | bytes 73732
  6.5 73.8 %reduce-scatter.9.cloned.1.call-start = ((), (), s32[]{:S(2)}) async-start(), calls=%async_computation.3 | async-start | bytes 491520
  17.7 23.2 %copy-start.3 = (u32[32]{0:T(128)S(1)}, u32[32]{0:T(128)}, u32[]{:S(2)}) copy-start(u32[32]{0:T(128)} %constant.83) | copy-start | bytes 388
  60.2 41.6 %reduce-scatter.7.cloned.1.call-start = ((), (), s32[]{:S(2)}) async-start(), calls=%async_computation.2 | async-start | bytes 491520
Sparse Core Ops, SparseCore 0:
  60.3 20.0 reduce-scatter.8
  82.7 19.0 reduce-scatter.6
